TPU v7x, 32 devices: a whole 2x2x4 slice. The times are simulated.
32 devices in a mesh: row: 4 (over z), col: 8 (over y, x, core).
Axes of the slice: x: 2, y: 2, z: 4, core: 2. Of those that a mesh axis runs over, the one named last changes fastest.
Arguments:
- child_inverse: bfloat16 [28672, 14336], P('row', 'col'), as said below
- root_upper: bfloat16 [20480, 20480], P('row', 'col'), as said below
- coupling: bfloat16 [4096, 28672], P('col', 'row'), may hold values from -0.046875 to 0.046875
- child_rhs: float32 [14336, 2, 128], P('col'), may hold values from -6 to 6
- root_rhs: float32 [20480, 128], P(('row', 'col')), may hold values from -6 to 6
- child_map: int32 [2, 32], replicated, may hold values from 0 to 159, as said below
Outputs:
- root_solution: float32 [20480, 128], P(('row', 'col'))
- child_solution: float32 [14336, 2, 128], P('col')
Inputs may be any that keep to these rules, and one draw needn't show every extreme that they name: `child_inverse`: for each child k, rows k * 14336 to (k + 1) * 14336 - 1 hold a lower triangular matrix: zero above the diagonal, diagonal entries between 0.5 and 1.5. `root_upper`: an upper triangular matrix: zero below the diagonal, diagonal entries between 0.5 and 1.5. `child_map`: each row lists 4096 / 128 distinct root blocks in increasing order, beginning with block 0 and ending with block 159.
All inputs are finite; a program needn't handle non-finite values.
Results may differ from a plain program's by a relative error of at most 0.018.
Values may be sent and summed in bfloat16 or wider, within the bound.
A program may use at most 192 MiB of HBM per device.

v0:
```python
import jax
import jax.numpy as jnp
from jax import lax
from jax.sharding import PartitionSpec as P

BLK = 128


def local(child_inverse, root_upper, coupling, child_rhs, root_rhs, child_map):
    row_devices = lax.axis_size("row")
    row_place = lax.axis_index("row")
    col_place = lax.axis_index("col")
    child_slot = row_place // (row_devices // 2)
    root_rows = root_upper.shape[0]
    coupled = coupling.shape[0]
    rhs_width = child_rhs.shape[2]
    slot_mask = jnp.arange(2, dtype=jnp.int32) == child_slot
    contract_first = (((0,), (0,)), ((), ()))
    own_rhs = lax.dynamic_index_in_dim(child_rhs, child_slot, 1, keepdims=False).astype(
        jnp.bfloat16
    )
    block = child_inverse
    child_solved = lax.psum(
        jnp.dot(block, own_rhs, preferred_element_type=jnp.float32).astype(jnp.bfloat16), "col"
    ).astype(jnp.float32)
    child_low = child_solved.astype(jnp.bfloat16)
    update = jnp.dot(coupling, child_low, preferred_element_type=jnp.float32)
    update_slots = jnp.where(slot_mask[:, None, None], update[None], 0.0)
    update_both = lax.psum(update_slots.astype(jnp.bfloat16), "row").astype(jnp.float32)
    per_col = coupled // BLK
    root_blocks = root_rows // BLK
    local_map = lax.dynamic_slice_in_dim(child_map, col_place * per_col, per_col, 1)
    target = local_map - row_place * root_blocks
    block_hits = target[:, :, None] == jnp.arange(root_blocks, dtype=jnp.int32)[None, None, :]
    placed = jnp.einsum(
        "kbj,kbpq->jpq",
        block_hits.astype(jnp.float32),
        update_both.reshape(2, per_col, BLK, rhs_width),
        precision=lax.Precision.HIGHEST,
    ).reshape(root_rows, rhs_width)
    rhs_rows = root_rhs.shape[0]
    given_rows = lax.dynamic_update_slice(
        jnp.zeros((root_rows, rhs_width), jnp.float32),
        root_rhs,
        (col_place * rhs_rows, jnp.int32(0)),
    )
    root_term = given_rows - placed
    root_low = lax.psum(root_term.astype(jnp.bfloat16), "col")
    columns = root_upper
    solved_low = lax.psum(
        lax.dot_general(
            columns, root_low, contract_first, preferred_element_type=jnp.float32
        ).astype(jnp.bfloat16),
        "row",
    )
    block = root_upper
    root_solution = lax.psum_scatter(
        jnp.dot(block, solved_low, preferred_element_type=jnp.float32).astype(jnp.bfloat16),
        "col",
        scatter_dimension=0,
        tiled=True,
    ).astype(jnp.float32)
    rows_low = lax.all_gather(root_solution.astype(jnp.bfloat16), "col", axis=0, tiled=True)
    picked = jnp.einsum(
        "kbj,jpq->kbpq",
        block_hits.astype(jnp.bfloat16),
        rows_low.reshape(root_blocks, BLK, rhs_width),
        preferred_element_type=jnp.float32,
    ).reshape(2, coupled, rhs_width)
    picked_both = lax.psum(picked.astype(jnp.bfloat16), "row").astype(jnp.float32)
    own_pick = lax.dynamic_index_in_dim(picked_both, child_slot, 0, keepdims=False).astype(
        jnp.bfloat16
    )
    columns = coupling
    back_term = lax.psum(
        lax.dot_general(
            columns, own_pick, contract_first, preferred_element_type=jnp.float32
        ).astype(jnp.bfloat16),
        "col",
    ).astype(jnp.float32)
    adjusted = (child_solved - back_term).astype(jnp.bfloat16)
    final_rows = lax.dot_general(
        child_inverse, adjusted, contract_first, preferred_element_type=jnp.float32
    )
    final_slots = jnp.where(slot_mask[None, :, None], final_rows[:, None, :], 0.0)
    child_solution = lax.psum(final_slots.astype(jnp.bfloat16), "row").astype(jnp.float32)
    return (root_solution, child_solution)


def solution(mesh):
    return jax.shard_map(
        local,
        mesh=mesh,
        in_specs=(
            P("row", "col"),
            P("row", "col"),
            P("col", "row"),
            P("col", None, None),
            P(("row", "col"), None),
            P(),
        ),
        out_specs=(P(("row", "col"), None), P("col", None, None)),
        check_vma=False,
    )
```

profile of v0, /device:TPU:0, one launch (start us, length us, event | category | flops | bytes accessed | tf_op | source)
XLA Modules:
  0.0 498.9 jit_solution(968148228895632408)
XLA Ops:
  7.2 1.4 copy-done
  9.5 14.6 %fusion.1 = bf16[7168,128]{0,1:T(8,128)(2,1)} fusion(bf16[7168,1792]{1,0:T(8,128)(2,1)} %param.6, f32[1792,1,128]{2,0,1:T(8,128)S(1)} %bitcast.52), kind=kOutput, calls=%fused_computation.3 | convolution fusion | flops 3289481216 | bytes 28442624 | tf_op jit(solution)/shard_map/dot_general | solution.py:24
  24.2 62.9 %all-reduce.8.cloned.1.call-done = bf16[7168,128]{0,1:T(8,128)(2,1)} async-done(((bf16[7168,128]{0,1:T(8,128)(2,1)}), bf16[7168,128]{0,1:T(8,128)(2,1)}) %all-reduce.8.cloned.1.call-update) | async-done | bytes 1835024 | tf_op jit(solution)/shard_map/psum | solution.py:23
  87.1 6.2 %convolution_bitcast_fusion.2 = bf16[512,128]{0,1:T(8,128)(2,1)S(1)} fusion(bf16[7168,128]{0,1:T(8,128)(2,1)} %all-reduce.8.cloned.1.call-done, bf16[512,7168]{1,0:T(8,128)(2,1)} %param.8), kind=kOutput, calls=%fused_computation.18 | convolution fusion | flops 939524096 | bytes 9306112 | tf_op jit(solution)/shard_map/dot_general | solution.py:27
  93.6 0.9 copy.29
  94.7 1.7 broadcast_in_dim.49
  97.1 32.5 %all-reduce.10.cloned.1.call-done = bf16[2,4,128,128]{3,1,0,2:T(4,128)(2,1)} async-done(((bf16[2,4,128,128]{3,1,0,2:T(4,128)(2,1)}), bf16[2,4,128,128]{3,1,0,2:T(4,128)(2,1)}) %all-reduce.10.cloned.1.call-update) | async-done | bytes 262160 | tf_op jit(solution)/shard_map/psum | solution.py:29
  129.6 1.6 convolution_bitcast_fusion.1
  131.7 3.0 fusion.4
  134.8 57.8 %all-reduce.12.cloned.1.call-done = bf16[5120,128]{1,0:T(8,128)(2,1)} async-done(((bf16[5120,128]{1,0:T(8,128)(2,1)}), bf16[5120,128]{1,0:T(8,128)(2,1)}) %all-reduce.12.cloned.1.call-update) | async-done | bytes 1310736 | tf_op jit(solution)/shard_map/psum | solution.py:48
  192.6 13.3 %fusion.3 = bf16[2560,128]{0,1:T(8,128)(2,1)} fusion(bf16[5120,128]{1,0:T(8,128)(2,1)} %all-reduce.12.cloned.1.call-done, bf16[5120,2560]{1,0:T(8,128)(2,1)} %param.7), kind=kOutput, calls=%fused_computation.8 | convolution fusion | flops 3355770880 | bytes 28180480 | tf_op jit(solution)/shard_map/dot_general | solution.py:51
  206.1 39.6 %all-reduce.14.cloned.1.call-done = bf16[2560,128]{0,1:T(8,128)(2,1)} async-done(((bf16[2560,128]{0,1:T(8,128)(2,1)}), bf16[2560,128]{0,1:T(8,128)(2,1)}) %all-reduce.14.cloned.1.call-update) | async-done | bytes 655376 | tf_op jit(solution)/shard_map/psum | solution.py:50
  245.7 13.4 %fusion.2 = bf16[5120,128]{0,1:T(8,128)(2,1)S(1)} fusion(bf16[2560,128]{0,1:T(8,128)(2,1)} %all-reduce.14.cloned.1.call-done, bf16[5120,2560]{1,0:T(8,128)(2,1)} %param.7), kind=kOutput, calls=%fused_computation.5 | convolution fusion | flops 3356098560 | bytes 28180480 | tf_op jit(solution)/shard_map/dot_general | solution.py:58
  259.1 1.4 copy.38
  260.6 36.8 %reduce-scatter.4.cloned.1.call-done = bf16[640,128]{1,0:T(8,128)(2,1)} async-done(((bf16[5120,128]{1,0:T(8,128)(2,1)}), bf16[640,128]{1,0:T(8,128)(2,1)}) %reduce-scatter.4.cloned.1.call-update) | async-done | bytes 163856 | tf_op jit(solution)/shard_map/reduce_scatter | solution.py:57
  297.5 26.2 %all-gather.2.cloned.1.call-done = bf16[5120,128]{1,0:T(8,128)(2,1)} async-done(((bf16[640,128]{1,0:T(8,128)(2,1)}), bf16[5120,128]{1,0:T(8,128)(2,1)}) %all-gather.2.cloned.1.call-update) | async-done | bytes 1310736 | tf_op jit(solution)/shard_map/all_gather | solution.py:63
  323.6 2.3 fusion.8
  326.7 35.7 %all-reduce.16.cloned.1.call-done = bf16[2,512,128]{2,1,0:T(8,128)(2,1)} async-done(((bf16[2,512,128]{2,1,0:T(8,128)(2,1)}), bf16[2,512,128]{2,1,0:T(8,128)(2,1)}) %all-reduce.16.cloned.1.call-update) | async-done | bytes 262160 | tf_op jit(solution)/shard_map/psum | solution.py:70
  362.4 5.5 %fusion = bf16[7168,128]{0,1:T(8,128)(2,1)} fusion(bf16[512,7168]{1,0:T(8,128)(2,1)} %param.8, bf16[2,512,128]{2,1,0:T(8,128)(2,1)} %all-reduce.16.cloned.1.call-done, s32[]{:T(128)S(6)} %select_n.28), kind=kOutput, calls=%fused_computation.2 | convolution fusion | flops 940572672 | bytes 9306116 | tf_op jit(solution)/shard_map/dot_general | solution.py:76
  368.0 60.1 %all-reduce.18.cloned.1.call-done = bf16[7168,128]{0,1:T(8,128)(2,1)} async-done(((bf16[7168,128]{0,1:T(8,128)(2,1)}), bf16[7168,128]{0,1:T(8,128)(2,1)}) %all-reduce.18.cloned.1.call-update) | async-done | bytes 1835024 | tf_op jit(solution)/shard_map/psum | solution.py:75
  428.1 12.4 %convolution_bitcast_fusion = bf16[1792,128]{0,1:T(8,128)(2,1)S(1)} fusion(bf16[7168,1792]{1,0:T(8,128)(2,1)} %param.6, bf16[7168,128]{0,1:T(8,128)(2,1)} %all-reduce.18.cloned.1.call-done, bf16[7168,128]{0,1:T(8,128)(2,1)S(1)} %copy-done.2), kind=kOutput, calls=%fused_computation.11 | convolution fusion | flops 3292004352 | bytes 29818880 | tf_op jit(solution)/shard_map/dot_general | solution.py:82
  440.8 1.6 select_convert_fusion
  443.5 46.2 %all-reduce.20.cloned.1.call-done = bf16[1792,2,128]{2,1,0:T(2,128)(2,1)} async-done(((bf16[1792,2,128]{2,1,0:T(2,128)(2,1)}), bf16[1792,2,128]{2,1,0:T(2,128)(2,1)}) %all-reduce.20.cloned.1.call-update) | async-done | bytes 917520 | tf_op jit(solution)/shard_map/psum | solution.py:86
  489.7 2.6 convert_element_type.96
  (40 shorter events, 5.1 us)
Async XLA Ops:
  7.2 1.5 copy-start
  7.2 79.9 %all-reduce.8.cloned.1.call-start = ((), (), s32[]{:S(2)}) async-start(), calls=%async_computation.1 | async-start | bytes 3670016 | tf_op jit(solution)/shard_map/psum | solution.py:23
  24.1 105.5 %all-reduce.10.cloned.1.call-start = ((), (), s32[]{:S(2)}) async-start(), calls=%async_computation.2 | async-start | bytes 524288 | tf_op jit(solution)/shard_map/psum | solution.py:29
  24.1 70.4 %copy-start.5 = (s32[2,32]{1,0:T(2,128)S(1)}, s32[2,32]{1,0:T(2,128)}, u32[]{:S(2)}) copy-start(s32[2,32]{1,0:T(2,128)} %param.11) | copy-start | bytes 772
  93.3 3.0 copy-start.4
  94.5 98.1 %all-reduce.12.cloned.1.call-start = ((), (), s32[]{:S(2)}) async-start(), calls=%async_computation.3 | async-start | bytes 2621440 | tf_op jit(solution)/shard_map/psum | solution.py:48
  134.8 110.9 %all-reduce.14.cloned.1.call-start = ((), (), s32[]{:S(2)}) async-start(), calls=%async_computation.4 | async-start | bytes 1310720 | tf_op jit(solution)/shard_map/psum | solution.py:50
  205.9 91.5 %reduce-scatter.4.cloned.1.call-start = ((), (), s32[]{:S(2)}) async-start(), calls=%async_computation.9 | async-start | bytes 1474560 | tf_op jit(solution)/shard_map/reduce_scatter | solution.py:57
  260.5 63.1 %all-gather.2.cloned.1.call-start = ((), (), s32[]{:S(2)}) async-start(), calls=%async_computation.5 | async-start | bytes 1474560 | tf_op jit(solution)/shard_map/all_gather | solution.py:63
  297.4 65.0 %all-reduce.16.cloned.1.call-start = ((), (), s32[]{:S(2)}) async-start(), calls=%async_computation.6 | async-start | bytes 524288 | tf_op jit(solution)/shard_map/psum | solution.py:70
  326.7 101.5 %all-reduce.18.cloned.1.call-start = ((), (), s32[]{:S(2)}) async-start(), calls=%async_computation.7 | async-start | bytes 3670016 | tf_op jit(solution)/shard_map/psum | solution.py:75
  368.0 60.2 %copy-start.2 = (bf16[7168,128]{0,1:T(8,128)(2,1)S(1)}, bf16[7168,128]{0,1:T(8,128)(2,1)}, u32[]{:S(2)}) copy-start(bf16[7168,128]{0,1:T(8,128)(2,1)} %all-reduce.8.cloned.1.call-done) | copy-start | bytes 5505028
  368.0 121.7 %all-reduce.20.cloned.1.call-start = ((), (), s32[]{:S(2)}) async-start(), calls=%async_computation.8 | async-start | bytes 1835008 | tf_op jit(solution)/shard_map/psum | solution.py:86
  440.5 2.0 copy-start.3
  440.5 51.8 %copy-start.1 = (f32[1792,2,128]{2,1,0:T(2,128)S(1)}, f32[1792,2,128]{2,1,0:T(2,128)}, u32[]{:S(2)}) copy-start(f32[1792,2,128]{2,1,0:T(2,128)} %param.9) | copy-start | bytes 5505028
Sparse Core Ops, SparseCore 0:
  24.2 62.8 all-reduce.7
  94.6 34.8 all-reduce.9
  134.9 57.6 all-reduce.11
  206.0 39.6 all-reduce.13
  260.6 36.7 reduce-scatter.3
  299.1 24.4 all-gather.1
  326.8 35.5 all-reduce.15
  368.1 59.9 all-reduce.17
  442.6 47.1 all-reduce.19
where the time goes:
time: 499 us
  waiting for transfers between devices  398 us (80%)
  matrix products  69.2 us (14%)
  between operations  14 us (3%)
  local copies, waits for them, and re-layouts  9.7 us (2%)
  other arithmetic  7.48 us (1%)
    psum x1, waiting for transfers between devices, local(): lax.psum(jnp.dot(block, own_rhs, preferred_element_type=jnp.float32).asty...  62.9 us
    psum x1, waiting for transfers between devices, local(): lax.psum(lax.dot_general(columns, own_pick, contract_first, preferred_ele...  60.1 us
    psum x1, waiting for transfers between devices, local(): root_low = lax.psum(root_term.astype(jnp.bfloat16), 'col')  57.8 us
    psum x1, waiting for transfers between devices, local(): lax.psum(final_slots.astype(jnp.bfloat16), 'row').astype(jnp.float32)  46.2 us
    psum x1, waiting for transfers between devices, local(): lax.psum(lax.dot_general(columns, root_low, contract_first, preferred_ele...  39.6 us
    reduce_scatter x1, waiting for transfers between devices, local(): lax.psum_scatter(jnp.dot(block, solved_low, preferred_element_type=jnp.fl...  36.8 us
    psum x1, waiting for transfers between devices, local(): lax.psum(picked.astype(jnp.bfloat16), 'row').astype(jnp.float32)  35.7 us
    psum x1, waiting for transfers between devices, local(): lax.psum(update_slots.astype(jnp.bfloat16), 'row').astype(jnp.float32)  32.5 us
  transfers between devices with their start and end apart: 9, of which 9 were waited for; matrix products, arithmetic and copies ran while one was open for 1% of the time, Pallas kernels for 0%

commit v1 on v0

v1 whole, which is shorter than its diff:
```python
import functools

import jax
import jax.numpy as jnp
from jax import lax
from jax.experimental import pallas as pl
from jax.experimental.pallas import tpu as pltpu
from jax.sharding import PartitionSpec as P

BLK = 128
MESH = pl.DeviceIdType.MESH


def bits_of(n):
    m = n.bit_length() - 1
    assert 1 << m == n
    return m


def greet(axis, me, bits):
    barrier = pltpu.get_barrier_semaphore()
    for b in bits:
        pl.semaphore_signal(
            barrier, inc=1, device_id={axis: me ^ (1 << b)}, device_id_type=MESH
        )
    pl.semaphore_wait(barrier, len(bits))


def remote(axis, me, bit, src, dst, send, recv):
    copy = pltpu.make_async_remote_copy(
        src_ref=src,
        dst_ref=dst,
        send_sem=send,
        recv_sem=recv,
        device_id={axis: me ^ (1 << bit)},
        device_id_type=MESH,
    )
    copy.start()
    return copy


def scatter_steps(axis, me, orders, n, x_ref, w_ref, r_ref, put, send, recv):
    streams = len(orders)
    steps = len(orders[0])
    low = [jnp.int32(0)] * streams
    size = n
    offset = 0
    copies = []
    for t in range(steps):
        half = size // 2
        src = x_ref if t == 0 else w_ref
        now = []
        for s in range(streams):
            mine = (me >> orders[s][t]) & 1
            keep = low[s] + mine * half
            away = low[s] + (1 - mine) * half
            copy = remote(
                axis,
                me,
                orders[s][t],
                src.at[s, pl.ds(away, half)],
                r_ref.at[s, pl.ds(offset, half)],
                send.at[s, t],
                recv.at[s, t],
            )
            now.append(copy)
            low[s] = keep
        for s in range(streams):
            now[s].wait_recv()

            def add(i, _, s=s, src=src, offset=offset, last=t == steps - 1):
                place = low[s] + i
                total = (
                    src[s, place].astype(jnp.float32) + r_ref[s, offset + i].astype(jnp.float32)
                ).astype(jnp.bfloat16)
                if last:
                    put(s, place, total)
                else:
                    w_ref[s, place] = total
                return 0

            lax.fori_loop(0, half, add, 0)
        copies += now
        size = half
        offset += half
    return low, copies


def all_sum_kernel(axis, n, orders, gathers, x_ref, o_ref, w_ref, r_ref, send, recv):
    me = lax.axis_index(axis)
    steps = len(orders[0])
    streams = len(orders)
    greet(axis, me, list(range(steps)))

    def put(s, place, value):
        o_ref[s, place] = value

    low, copies = scatter_steps(axis, me, orders, n, x_ref, w_ref, r_ref, put, send, recv)
    size = 1
    for g in range(gathers):
        t = steps - 1 - g
        now = []
        for s in range(streams):
            part = o_ref.at[s, pl.ds(low[s], size)]
            now.append(
                remote(
                    axis, me, orders[s][t], part, part,
                    send.at[s, steps + g], recv.at[s, steps + g],
                )
            )
            low[s] = low[s] - ((me >> orders[s][t]) & 1) * size
        for copy in now:
            copy.wait_recv()
        copies += now
        size *= 2
    for copy in copies:
        copy.wait_send()


def all_sum(x, axis, n, orders, cid, gathers=None):
    rows, width = x.shape
    m = bits_of(n)
    gathers = m if gathers is None else gathers
    streams = len(orders)
    shape = (streams, n, rows // (streams * n), width)
    out = pl.pallas_call(
        functools.partial(all_sum_kernel, axis, n, orders, gathers),
        out_shape=jax.ShapeDtypeStruct(shape, jnp.bfloat16),
        in_specs=[pl.BlockSpec(memory_space=pltpu.VMEM)],
        out_specs=pl.BlockSpec(memory_space=pltpu.VMEM),
        scratch_shapes=[
            pltpu.VMEM(shape, jnp.bfloat16),
            pltpu.VMEM(shape, jnp.bfloat16),
            pltpu.SemaphoreType.DMA((streams, 2 * m)),
            pltpu.SemaphoreType.DMA((streams, 2 * m)),
        ],
        compiler_params=pltpu.CompilerParams(collective_id=cid, has_side_effects=True),
    )(x.reshape(shape))
    return out.reshape(rows, width)


def both_sum_kernel(axis, n, x_ref, o_ref, w_ref, r_ref, send, recv):
    me = lax.axis_index(axis)
    m = bits_of(n)
    slot = me >> (m - 1)
    greet(axis, me, list(range(m)))

    def put(s, place, value):
        o_ref[slot, place] = value

    order = list(range(m - 1))
    low, copies = scatter_steps(
        axis, me, [order], n // 2, x_ref, w_ref, r_ref, put, send, recv
    )
    place = low[0]
    part = o_ref.at[slot, pl.ds(place, 1)]
    cross = remote(axis, me, m - 1, part, part, send.at[0, m - 1], recv.at[0, m - 1])
    cross.wait_recv()
    copies.append(cross)
    size = 1
    for g in range(m - 1):
        bit = order[m - 2 - g]
        part = o_ref.at[:, pl.ds(place, size)]
        copy = remote(axis, me, bit, part, part, send.at[0, m + g], recv.at[0, m + g])
        place = place - ((me >> bit) & 1) * size
        copy.wait_recv()
        copies.append(copy)
        size *= 2
    for copy in copies:
        copy.wait_send()


def both_sum(x, axis, n, cid):
    rows, width = x.shape
    m = bits_of(n)
    half = n // 2
    chunk = rows // half
    out = pl.pallas_call(
        functools.partial(both_sum_kernel, axis, n),
        out_shape=jax.ShapeDtypeStruct((2, half, chunk, width), jnp.bfloat16),
        in_specs=[pl.BlockSpec(memory_space=pltpu.VMEM)],
        out_specs=pl.BlockSpec(memory_space=pltpu.VMEM),
        scratch_shapes=[
            pltpu.VMEM((1, half, chunk, width), jnp.bfloat16),
            pltpu.VMEM((1, half, chunk, width), jnp.bfloat16),
            pltpu.SemaphoreType.DMA((1, 2 * m)),
            pltpu.SemaphoreType.DMA((1, 2 * m)),
        ],
        compiler_params=pltpu.CompilerParams(collective_id=cid, has_side_effects=True),
    )(x.reshape(1, half, chunk, width))
    return out.reshape(2, rows, width)


def place_kernel(idx_ref, update_ref, given_ref, o_ref):
    def body(j, _):
        value = given_ref[j]
        for k in range(2):
            i = idx_ref[k, j]
            block = update_ref[jnp.maximum(i, 0)].astype(jnp.float32)
            value = value - jnp.where(i >= 0, block, 0.0)
        o_ref[j] = value.astype(jnp.bfloat16)
        return 0

    lax.fori_loop(0, o_ref.shape[0], body, 0)


def pick_kernel(idx_ref, rows_ref, o_ref):
    def body(j, _):
        i = idx_ref[j]
        block = rows_ref[jnp.maximum(i, 0)].astype(jnp.float32)
        o_ref[j] = jnp.where(i >= 0, block, 0.0).astype(jnp.bfloat16)
        return 0

    lax.fori_loop(0, o_ref.shape[0], body, 0)


def local(row_devices, col_devices, child_inverse, root_upper, coupling, child_rhs, root_rhs, child_map):
    row_place = lax.axis_index("row")
    col_place = lax.axis_index("col")
    child_slot = row_place // (row_devices // 2)
    root_rows = root_upper.shape[0]
    coupled = coupling.shape[0]
    rhs_width = child_rhs.shape[2]
    vmem = pl.BlockSpec(memory_space=pltpu.VMEM)
    smem = pl.BlockSpec(memory_space=pltpu.SMEM)
    row_bits = list(range(bits_of(row_devices)))
    col_bits = list(range(bits_of(col_devices)))
    col_orders = [col_bits, col_bits[:1] + col_bits[:0:-1]]
    row_orders = [row_bits, row_bits[::-1]]
    pick_order = [row_bits[-1:] + row_bits[:-1]]
    contract_first = (((0,), (0,)), ((), ()))

    per_col = coupled // BLK
    root_blocks = root_rows // BLK
    local_map = lax.dynamic_slice_in_dim(child_map, col_place * per_col, per_col, 1)
    target = local_map - row_place * root_blocks
    block_hits = target[:, :, None] == jnp.arange(root_blocks, dtype=jnp.int32)[None, None, :]
    slots = jnp.arange(2 * per_col, dtype=jnp.int32).reshape(2, per_col, 1)
    place_idx = jnp.max(jnp.where(block_hits, slots, -1), axis=1)
    pick_idx = jnp.where((target >= 0) & (target < root_blocks), target, -1).reshape(-1)
    rhs_rows = root_rhs.shape[0]
    given_rows = lax.dynamic_update_slice(
        jnp.zeros((root_rows, rhs_width), jnp.float32),
        root_rhs,
        (col_place * rhs_rows, jnp.int32(0)),
    )

    own_rhs = lax.dynamic_index_in_dim(child_rhs, child_slot, 1, keepdims=False).astype(
        jnp.bfloat16
    )
    child_low = all_sum(
        jnp.dot(child_inverse, own_rhs, preferred_element_type=jnp.float32).astype(jnp.bfloat16),
        "col", col_devices, col_orders, 0,
    )
    update = jnp.dot(coupling, child_low, preferred_element_type=jnp.float32)
    update_both = both_sum(update.astype(jnp.bfloat16), "row", row_devices, 1)
    root_term = pl.pallas_call(
        place_kernel,
        out_shape=jax.ShapeDtypeStruct((root_blocks, BLK, rhs_width), jnp.bfloat16),
        in_specs=[smem, vmem, vmem],
        out_specs=vmem,
    )(
        place_idx,
        update_both.reshape(2 * per_col, BLK, rhs_width),
        given_rows.reshape(root_blocks, BLK, rhs_width),
    )
    root_low = all_sum(
        root_term.reshape(root_rows, rhs_width), "col", col_devices, col_orders, 2
    )
    solved_low = all_sum(
        lax.dot_general(
            root_upper, root_low, contract_first, preferred_element_type=jnp.float32
        ).astype(jnp.bfloat16),
        "row", row_devices, row_orders, 3,
    )
    rows_low = all_sum(
        jnp.dot(root_upper, solved_low, preferred_element_type=jnp.float32).astype(jnp.bfloat16),
        "col", col_devices, col_orders, 4,
    )
    root_solution = lax.dynamic_slice_in_dim(rows_low, col_place * rhs_rows, rhs_rows, 0).astype(
        jnp.float32
    )
    picked = pl.pallas_call(
        pick_kernel,
        out_shape=jax.ShapeDtypeStruct((2 * per_col, BLK, rhs_width), jnp.bfloat16),
        in_specs=[smem, vmem],
        out_specs=vmem,
    )(pick_idx, rows_low.reshape(root_blocks, BLK, rhs_width))
    picked_half = all_sum(
        picked.reshape(2 * coupled, rhs_width), "row", row_devices, pick_order, 5,
        gathers=len(row_bits) - 1,
    )
    own_pick = lax.dynamic_slice_in_dim(picked_half, child_slot * coupled, coupled, 0)
    back_term = all_sum(
        lax.dot_general(
            coupling, own_pick, contract_first, preferred_element_type=jnp.float32
        ).astype(jnp.bfloat16),
        "col", col_devices, col_orders, 6,
    )
    adjusted = (child_low.astype(jnp.float32) - back_term.astype(jnp.float32)).astype(
        jnp.bfloat16
    )
    final_rows = lax.dot_general(
        child_inverse, adjusted, contract_first, preferred_element_type=jnp.float32
    )
    final_both = both_sum(final_rows.astype(jnp.bfloat16), "row", row_devices, 7)
    child_solution = jnp.transpose(final_both, (1, 0, 2)).astype(jnp.float32)
    return (root_solution, child_solution)


def solution(mesh):
    return jax.shard_map(
        functools.partial(local, mesh.shape["row"], mesh.shape["col"]),
        mesh=mesh,
        in_specs=(
            P("row", "col"),
            P("row", "col"),
            P("col", "row"),
            P("col", None, None),
            P(("row", "col"), None),
            P(),
        ),
        out_specs=(P(("row", "col"), None), P("col", None, None)),
        check_vma=False,
    )
```

time: 499 us -> 301 us (0.60)
  waiting for transfers between devices: 398 us -> 0 us
  Pallas kernels: 0 us -> 212 us
  between operations: 14 us -> 0.81 us
  local copies, waits for them, and re-layouts: 9.7 us -> 20.5 us
  matrix products: 69.2 us -> 62.6 us
    psum x7 -> x0, waiting for transfers between devices: 335 us -> none  [the longest x1 62.9 us: local(): lax.psum(jnp.dot(block, own_rhs, preferred_element_type=jnp.float32).asty...]
    pallas_call x0 -> x10, Pallas kernels: none -> 212 us  [the longest x6 160 us: all_sum(): pl.pallas_call(functools.partial(all_sum_kernel, axis, n, orders, gathers...]
    reduce_scatter x1 -> x0, waiting for transfers between devices: 36.8 us -> none  [local(): lax.psum_scatter(jnp.dot(block, solved_low, preferred_element_type=jnp.fl...]
    all_gather x1 -> x0, waiting for transfers between devices: 26.2 us -> none  [local(): lax.all_gather(root_solution.astype(jnp.bfloat16), 'col', axis=0, tiled=T...]
    convert_element_type x1 -> x7, local copies, waits for them, and re-layouts: 0.74 us -> 16.6 us  [the longest x1 7.79 us: local(): child_solution = jnp.transpose(final_both, (1, 0, 2)).astype(jnp.float32)]
    dot_general x6 -> x4, matrix products: 50.6 us -> 44 us  [the longest x1 13.8 us: local(): jnp.dot(root_upper, solved_low, preferred_element_type=jnp.float32)]
  transfers between devices with their start and end apart: 9 -> 0, of which waited for: 9 -> 0; matrix products, arithmetic and copies ran while one was open for 1% -> 0% of each run, Pallas kernels for 0% -> 0%
where the time goes in v1:
time: 301 us; the launch traced here: 300 us
  Pallas kernels  212 us (70%)
  matrix products  62.6 us (21%)
  local copies, waits for them, and re-layouts  20.5 us (7%)
  other arithmetic  4.59 us (2%)
    pallas_call x6, Pallas kernels, all_sum(): pl.pallas_call(functools.partial(all_sum_kernel, axis, n, orders, gathers...  160 us
    pallas_call x2, Pallas kernels, both_sum(): pl.pallas_call(functools.partial(both_sum_kernel, axis, n), out_shape=jax...  46 us
    dot_general x1, matrix products, local(): jnp.dot(root_upper, solved_low, preferred_element_type=jnp.float32)  13.8 us
    dot_general x1, matrix products, local(): jnp.dot(child_inverse, own_rhs, preferred_element_type=jnp.float32)  13.3 us
    dot_general x1, matrix products, local(): lax.dot_general(root_upper, root_low, contract_first, preferred_element_t...  12.4 us
    dot_general x1, matrix products, local(): lax.dot_general(child_inverse, adjusted, contract_first, preferred_elemen...  12.4 us
    convert_element_type x1, local copies, waits for them, and re-layouts, local(): child_solution = jnp.transpose(final_both, (1, 0, 2)).astype(jnp.float32)  7.79 us
    dot_general x1, matrix products, local(): update = jnp.dot(coupling, child_low, preferred_element_type=jnp.float32)  6.22 us

profile of v1, /device:TPU:0, one launch (start us, length us, event | category | flops | bytes accessed | tf_op | source)
XLA Modules:
  0.0 300.3 jit_solution(269264113981300455)
XLA Ops:
  3.6 13.3 %fusion.1 = bf16[7168,128]{0,1:T(8,128)(2,1)S(1)} fusion(bf16[7168,1792]{1,0:T(8,128)(2,1)} %param.6, f32[1792,1,128]{2,0,1:T(8,128)S(1)} %bitcast.59), kind=kOutput, calls=%fused_computation.3 | convolution fusion | flops 3289481216 | bytes 28442624 | tf_op jit(solution)/shard_map/dot_general | solution.py:252
  17.0 2.3 copy.24
  19.3 30.9 %shard_map.77 = bf16[2,8,448,128]{3,2,1,0:T(8,128)(2,1)} custom-call(bf16[2,8,448,128]{3,2,1,0:T(8,128)(2,1)} %bitcast.52), custom_call_target="tpu_custom_call" | custom-call | tf_op jit(solution)/shard_map/pallas_call | solution.py:126
  50.2 6.2 %fusion.7 = bf16[512,128]{0,1:T(8,128)(2,1)S(1)} fusion(bf16[7168,128]{1,0:T(8,128)(2,1)} %bitcast.49, bf16[512,7168]{1,0:T(8,128)(2,1)} %param.8), kind=kOutput, calls=%fused_computation.14 | convolution fusion | flops 939589632 | bytes 9306112 | tf_op jit(solution)/shard_map/dot_general | solution.py:255
  57.2 15.4 %shard_map.78 = bf16[2,2,256,128]{3,2,1,0:T(8,128)(2,1)} custom-call(bf16[1,2,256,128]{3,2,1,0:T(8,128)(2,1)} %bitcast.67), custom_call_target="tpu_custom_call" | custom-call | tf_op jit(solution)/shard_map/pallas_call | solution.py:178
  72.6 1.7 broadcast_in_dim.23
  75.1 3.9 %shard_map.79 = bf16[40,128,128]{2,1,0:T(8,128)(2,1)} custom-call(s32[2,40]{1,0:T(2,128)} %select_reduce_fusion.idx_ref, bf16[8,128,128]{2,1,0:T(8,128)(2,1)} %bitcast.64, f32[40,128,128]{2,1,0:T(8,128)} %bitcast.7.given_ref), custom_call_target="tpu_custom_call" | custom-call | tf_op jit(solution)/shard_map/pallas_call | solution.py:257
  78.9 24.6 %shard_map.80 = bf16[2,8,320,128]{3,2,1,0:T(8,128)(2,1)} custom-call(bf16[2,8,320,128]{3,2,1,0:T(8,128)(2,1)} %bitcast.57), custom_call_target="tpu_custom_call" | custom-call | tf_op jit(solution)/shard_map/pallas_call | solution.py:126
  103.6 12.4 %fusion.4 = bf16[2560,128]{0,1:T(8,128)(2,1)S(1)} fusion(bf16[5120,128]{1,0:T(8,128)(2,1)} %bitcast.54, bf16[5120,2560]{1,0:T(8,128)(2,1)} %param.7), kind=kOutput, calls=%fused_computation.9 | convolution fusion | flops 3355770880 | bytes 28180480 | tf_op jit(solution)/shard_map/dot_general | solution.py:271
  116.0 1.1 copy.26
  117.1 32.6 %shard_map.81 = bf16[2,4,320,128]{3,2,1,0:T(8,128)(2,1)} custom-call(bf16[2,4,320,128]{3,2,1,0:T(8,128)(2,1)} %bitcast.61), custom_call_target="tpu_custom_call" | custom-call | tf_op jit(solution)/shard_map/pallas_call | solution.py:126
  149.7 13.8 %fusion.2 = bf16[5120,128]{0,1:T(8,128)(2,1)S(1)} fusion(bf16[2560,128]{1,0:T(8,128)(2,1)} %bitcast.60, bf16[5120,2560]{1,0:T(8,128)(2,1)} %param.7), kind=kOutput, calls=%fused_computation.5 | convolution fusion | flops 3356098560 | bytes 28180480 | tf_op jit(solution)/shard_map/dot_general | solution.py:277
  163.6 1.4 copy.27
  165.0 24.0 %shard_map.82 = bf16[2,8,320,128]{3,2,1,0:T(8,128)(2,1)} custom-call(bf16[2,8,320,128]{3,2,1,0:T(8,128)(2,1)} %bitcast.58), custom_call_target="tpu_custom_call" | custom-call | tf_op jit(solution)/shard_map/pallas_call | solution.py:126
  189.0 2.1 shard_map.83
  191.2 17.7 %shard_map.84 = bf16[1,4,256,128]{3,2,1,0:T(8,128)(2,1)} custom-call(bf16[1,4,256,128]{3,2,1,0:T(8,128)(2,1)} %bitcast.65), custom_call_target="tpu_custom_call" | custom-call | tf_op jit(solution)/shard_map/pallas_call | solution.py:126
  208.9 1.7 dynamic-slice_convert_fusion
  210.6 4.3 %fusion = bf16[7168,128]{0,1:T(8,128)(2,1)S(1)} fusion(bf16[512,7168]{1,0:T(8,128)(2,1)} %param.8, bf16[1024,128]{1,0:T(8,128)(2,1)} %bitcast.66, s32[]{:T(128)S(6)} %select_n.33), kind=kOutput, calls=%fused_computation.2 | convolution fusion | flops 940441600 | bytes 9306116 | tf_op jit(solution)/shard_map/dot_general | solution.py:295
  214.9 2.3 copy.28
  217.2 29.8 %shard_map.85 = bf16[2,8,448,128]{3,2,1,0:T(8,128)(2,1)} custom-call(bf16[2,8,448,128]{3,2,1,0:T(8,128)(2,1)} %bitcast.53), custom_call_target="tpu_custom_call" | custom-call | tf_op jit(solution)/shard_map/pallas_call | solution.py:126
  247.1 12.4 %fusion.5 = bf16[1792,128]{0,1:T(8,128)(2,1)S(1)} fusion(bf16[7168,1792]{1,0:T(8,128)(2,1)} %param.6, bf16[7168,128]{1,0:T(8,128)(2,1)} %bitcast.51, bf16[7168,128]{1,0:T(8,128)(2,1)S(1)} %bitcast.50), kind=kOutput, calls=%fused_computation.11 | convolution fusion | flops 3292233728 | bytes 29818880 | tf_op jit(solution)/shard_map/dot_general | solution.py:303
  260.5 30.6 %shard_map.86 = bf16[2,2,896,128]{3,2,1,0:T(8,128)(2,1)} custom-call(bf16[1,2,896,128]{3,2,1,0:T(8,128)(2,1)} %bitcast.63), custom_call_target="tpu_custom_call" | custom-call | tf_op jit(solution)/shard_map/pallas_call | solution.py:178
  291.1 1.4 bitcast_convert_fusion
  292.5 7.8 %copy.33 = f32[2,1792,128]{2,0,1:T(2,128)} copy(f32[2,1792,128]{2,1,0:T(8,128)S(1)} %bitcast_convert_fusion) | data formatting | bytes 3670016 | tf_op jit(solution)/shard_map/convert_element_type | solution.py:307
  (15 shorter events, 5.4 us)
Async XLA Ops:
  0.6 2.2 copy-start
  56.5 17.9 %copy-start.3 = (f32[640,128]{1,0:T(8,128)S(1)}, f32[640,128]{1,0:T(8,128)}, u32[]{:S(2)}) copy-start(f32[640,128]{1,0:T(8,128)} %param.10) | copy-start | bytes 983044
  217.2 29.8 %copy-start.2 = (bf16[2,8,448,128]{3,2,1,0:T(8,128)(2,1)S(1)}, bf16[2,8,448,128]{3,2,1,0:T(8,128)(2,1)}, u32[]{:S(2)}) copy-start(bf16[2,8,448,128]{3,2,1,0:T(8,128)(2,1)} %shard_map.77) | copy-start | bytes 5505028
  291.0 9.2 %copy-start.1 = (f32[1792,2,128]{2,1,0:T(2,128)S(1)}, f32[1792,2,128]{2,1,0:T(2,128)}, u32[]{:S(2)}) copy-start(f32[1792,2,128]{2,1,0:T(2,128)} %param.9) | copy-start | bytes 5505028

commit v2 on v1

--- a/solution.py
+++ b/solution.py
@@ -39,82 +39,74 @@
     return copy
 
 
-def scatter_steps(axis, me, orders, n, x_ref, w_ref, r_ref, put, send, recv):
-    streams = len(orders)
-    steps = len(orders[0])
-    low = [jnp.int32(0)] * streams
+def run_streams(streams, steps, begin, finish):
+    copies = [[begin(s, 0)] for s in range(streams)]
+    for t in range(steps):
+        for s in range(streams):
+            copies[s][t].wait_recv()
+            finish(s, t)
+            if t + 1 < steps:
+                copies[s].append(begin(s, t + 1))
+    for own in copies:
+        for copy in own:
+            copy.wait_send()
+
+
+def spans(me, order, n):
+    low = jnp.int32(0)
     size = n
     offset = 0
-    copies = []
-    for t in range(steps):
+    out = []
+    for b in order:
         half = size // 2
-        src = x_ref if t == 0 else w_ref
-        now = []
-        for s in range(streams):
-            mine = (me >> orders[s][t]) & 1
-            keep = low[s] + mine * half
-            away = low[s] + (1 - mine) * half
-            copy = remote(
-                axis,
-                me,
-                orders[s][t],
-                src.at[s, pl.ds(away, half)],
-                r_ref.at[s, pl.ds(offset, half)],
-                send.at[s, t],
-                recv.at[s, t],
-            )
-            now.append(copy)
-            low[s] = keep
-        for s in range(streams):
-            now[s].wait_recv()
-
-            def add(i, _, s=s, src=src, offset=offset, last=t == steps - 1):
-                place = low[s] + i
-                total = (
-                    src[s, place].astype(jnp.float32) + r_ref[s, offset + i].astype(jnp.float32)
-                ).astype(jnp.bfloat16)
-                if last:
-                    put(s, place, total)
-                else:
-                    w_ref[s, place] = total
-                return 0
-
-            lax.fori_loop(0, half, add, 0)
-        copies += now
-        size = half
-        offset += half
-    return low, copies
+        mine = (me >> b) & 1
+        keep, away = low + mine * half, low + (1 - mine) * half
+        out.append((keep, away, half, offset))
+        low, size, offset = keep, half, offset + half
+    return out
+
+
+def add_landed(s, span, src, r_ref, put):
+    keep, _, half, offset = span
+
+    def add(i, _):
+        total = src[s, keep + i].astype(jnp.float32) + r_ref[s, offset + i].astype(jnp.float32)
+        put(keep + i, total.astype(jnp.bfloat16))
+        return 0
+
+    lax.fori_loop(0, half, add, 0)
 
 
 def all_sum_kernel(axis, n, orders, gathers, x_ref, o_ref, w_ref, r_ref, send, recv):
     me = lax.axis_index(axis)
     steps = len(orders[0])
-    streams = len(orders)
+    plans = [spans(me, order, n) for order in orders]
     greet(axis, me, list(range(steps)))
 
-    def put(s, place, value):
-        o_ref[s, place] = value
-
-    low, copies = scatter_steps(axis, me, orders, n, x_ref, w_ref, r_ref, put, send, recv)
-    size = 1
-    for g in range(gathers):
-        t = steps - 1 - g
-        now = []
-        for s in range(streams):
-            part = o_ref.at[s, pl.ds(low[s], size)]
-            now.append(
-                remote(
-                    axis, me, orders[s][t], part, part,
-                    send.at[s, steps + g], recv.at[s, steps + g],
-                )
-            )
-            low[s] = low[s] - ((me >> orders[s][t]) & 1) * size
-        for copy in now:
-            copy.wait_recv()
-        copies += now
-        size *= 2
-    for copy in copies:
-        copy.wait_send()
+    def begin(s, t):
+        if t < steps:
+            _, away, half, offset = plans[s][t]
+            src = (x_ref if t == 0 else w_ref).at[s, pl.ds(away, half)]
+            dst = r_ref.at[s, pl.ds(offset, half)]
+            bit = orders[s][t]
+        else:
+            back = 2 * steps - 1 - t
+            src = dst = o_ref.at[s, pl.ds(plans[s][back][0], plans[s][back][2])]
+            bit = orders[s][back]
+        return remote(axis, me, bit, src, dst, send.at[s, t], recv.at[s, t])
+
+    def finish(s, t):
+        if t < steps:
+
+            def put(place, value):
+                if t == steps - 1:
+                    o_ref[s, place] = value
+                else:
+                    w_ref[s, place] = value
+
+            add_landed(s, plans[s][t], x_ref if t == 0 else w_ref, r_ref, put)
+
+    run_streams(len(orders), steps + gathers, begin, finish)
 
 
 def all_sum(x, axis, n, orders, cid, gathers=None):
@@ -139,55 +131,59 @@
     return out.reshape(rows, width)
 
 
-def both_sum_kernel(axis, n, x_ref, o_ref, w_ref, r_ref, send, recv):
+def both_sum_kernel(axis, n, streams, x_ref, o_ref, w_ref, r_ref, send, recv):
     me = lax.axis_index(axis)
     m = bits_of(n)
     slot = me >> (m - 1)
+    plan = spans(me, list(range(m - 1)), n // 2)
     greet(axis, me, list(range(m)))
 
-    def put(s, place, value):
-        o_ref[slot, place] = value
-
-    order = list(range(m - 1))
-    low, copies = scatter_steps(
-        axis, me, [order], n // 2, x_ref, w_ref, r_ref, put, send, recv
-    )
-    place = low[0]
-    part = o_ref.at[slot, pl.ds(place, 1)]
-    cross = remote(axis, me, m - 1, part, part, send.at[0, m - 1], recv.at[0, m - 1])
-    cross.wait_recv()
-    copies.append(cross)
-    size = 1
-    for g in range(m - 1):
-        bit = order[m - 2 - g]
-        part = o_ref.at[:, pl.ds(place, size)]
-        copy = remote(axis, me, bit, part, part, send.at[0, m + g], recv.at[0, m + g])
-        place = place - ((me >> bit) & 1) * size
-        copy.wait_recv()
-        copies.append(copy)
-        size *= 2
-    for copy in copies:
-        copy.wait_send()
-
-
-def both_sum(x, axis, n, cid):
+    def begin(s, t):
+        if t < m - 1:
+            _, away, half, offset = plan[t]
+            src = (x_ref if t == 0 else w_ref).at[s, pl.ds(away, half)]
+            dst = r_ref.at[s, pl.ds(offset, half)]
+            bit = t
+        elif t == m - 1:
+            src = dst = o_ref.at[slot, s, pl.ds(plan[-1][0], 1)]
+            bit = m - 1
+        else:
+            bit = 2 * (m - 1) - t
+            src = dst = o_ref.at[:, s, pl.ds(plan[bit][0], plan[bit][2])]
+        return remote(axis, me, bit, src, dst, send.at[s, t], recv.at[s, t])
+
+    def finish(s, t):
+        if t < m - 1:
+
+            def put(place, value):
+                if t == m - 2:
+                    o_ref[slot, s, place] = value
+                else:
+                    w_ref[s, place] = value
+
+            add_landed(s, plan[t], x_ref if t == 0 else w_ref, r_ref, put)
+
+    run_streams(streams, 2 * m - 1, begin, finish)
+
+
+def both_sum(x, axis, n, streams, cid):
     rows, width = x.shape
     m = bits_of(n)
     half = n // 2
-    chunk = rows // half
+    shape = (streams, half, rows // (streams * half), width)
     out = pl.pallas_call(
-        functools.partial(both_sum_kernel, axis, n),
-        out_shape=jax.ShapeDtypeStruct((2, half, chunk, width), jnp.bfloat16),
+        functools.partial(both_sum_kernel, axis, n, streams),
+        out_shape=jax.ShapeDtypeStruct((2,) + shape, jnp.bfloat16),
         in_specs=[pl.BlockSpec(memory_space=pltpu.VMEM)],
         out_specs=pl.BlockSpec(memory_space=pltpu.VMEM),
         scratch_shapes=[
-            pltpu.VMEM((1, half, chunk, width), jnp.bfloat16),
-            pltpu.VMEM((1, half, chunk, width), jnp.bfloat16),
-            pltpu.SemaphoreType.DMA((1, 2 * m)),
-            pltpu.SemaphoreType.DMA((1, 2 * m)),
+            pltpu.VMEM(shape, jnp.bfloat16),
+            pltpu.VMEM(shape, jnp.bfloat16),
+            pltpu.SemaphoreType.DMA((streams, 2 * m)),
+            pltpu.SemaphoreType.DMA((streams, 2 * m)),
         ],
         compiler_params=pltpu.CompilerParams(collective_id=cid, has_side_effects=True),
-    )(x.reshape(1, half, chunk, width))
+    )(x.reshape(shape))
     return out.reshape(2, rows, width)
 
 
@@ -225,8 +221,8 @@
     smem = pl.BlockSpec(memory_space=pltpu.SMEM)
     row_bits = list(range(bits_of(row_devices)))
     col_bits = list(range(bits_of(col_devices)))
-    col_orders = [col_bits, col_bits[:1] + col_bits[:0:-1]]
-    row_orders = [row_bits, row_bits[::-1]]
+    col_orders = [col_bits, col_bits[:1] + col_bits[:0:-1]] * 2
+    row_orders = [row_bits, row_bits[::-1]] * 2
     pick_order = [row_bits[-1:] + row_bits[:-1]]
     contract_first = (((0,), (0,)), ((), ()))
 
@@ -253,7 +249,7 @@
         "col", col_devices, col_orders, 0,
     )
     update = jnp.dot(coupling, child_low, preferred_element_type=jnp.float32)
-    update_both = both_sum(update.astype(jnp.bfloat16), "row", row_devices, 1)
+    update_both = both_sum(update.astype(jnp.bfloat16), "row", row_devices, 2, 1)
     root_term = pl.pallas_call(
         place_kernel,
         out_shape=jax.ShapeDtypeStruct((root_blocks, BLK, rhs_width), jnp.bfloat16),
@@ -303,7 +299,7 @@
     final_rows = lax.dot_general(
         child_inverse, adjusted, contract_first, preferred_element_type=jnp.float32
     )
-    final_both = both_sum(final_rows.astype(jnp.bfloat16), "row", row_devices, 7)
+    final_both = both_sum(final_rows.astype(jnp.bfloat16), "row", row_devices, 4, 7)
     child_solution = jnp.transpose(final_both, (1, 0, 2)).astype(jnp.float32)
     return (root_solution, child_solution)
 

time: 301 us -> 277 us (0.920)
  Pallas kernels: 212 us -> 188 us
    pallas_call x6, Pallas kernels: 160 us -> 142 us  [all_sum(): pl.pallas_call(functools.partial(all_sum_kernel, axis, n, orders, gathers...]
    pallas_call x2, Pallas kernels: 46 us -> 40.2 us  [both_sum(): pl.pallas_call(functools.partial(both_sum_kernel, axis, n, streams), out_...]
where the time goes in v2:
time: 277 us
  Pallas kernels  188 us (68%)
  matrix products  62.6 us (23%)
  local copies, waits for them, and re-layouts  20.5 us (7%)
  other arithmetic  4.59 us (2%)
    pallas_call x6, Pallas kernels, all_sum(): pl.pallas_call(functools.partial(all_sum_kernel, axis, n, orders, gathers...  142 us
    pallas_call x2, Pallas kernels, both_sum(): pl.pallas_call(functools.partial(both_sum_kernel, axis, n, streams), out_...  40.2 us
    dot_general x1, matrix products, local(): jnp.dot(root_upper, solved_low, preferred_element_type=jnp.float32)  13.8 us
    dot_general x1, matrix products, local(): jnp.dot(child_inverse, own_rhs, preferred_element_type=jnp.float32)  13.3 us
    dot_general x1, matrix products, local(): lax.dot_general(root_upper, root_low, contract_first, preferred_element_t...  12.4 us
    dot_general x1, matrix products, local(): lax.dot_general(child_inverse, adjusted, contract_first, preferred_elemen...  12.4 us
    convert_element_type x1, local copies, waits for them, and re-layouts, local(): child_solution = jnp.transpose(final_both, (1, 0, 2)).astype(jnp.float32)  7.79 us
    dot_general x1, matrix products, local(): update = jnp.dot(coupling, child_low, preferred_element_type=jnp.float32)  6.21 us

profile of v2, /device:TPU:0, one launch (start us, length us, event | category | flops | bytes accessed | tf_op | source)
XLA Modules:
  0.0 276.5 jit_solution(2039595361303731923)
XLA Ops:
  3.6 13.3 %fusion.1 = bf16[7168,128]{0,1:T(8,128)(2,1)S(1)} fusion(bf16[7168,1792]{1,0:T(8,128)(2,1)} %param.6, f32[1792,1,128]{2,0,1:T(8,128)S(1)} %bitcast.59), kind=kOutput, calls=%fused_computation.3 | convolution fusion | flops 3289481216 | bytes 28442624 | tf_op jit(solution)/shard_map/dot_general | solution.py:248
  17.0 2.3 copy.24
  19.3 28.0 %shard_map.77 = bf16[4,8,224,128]{3,2,1,0:T(8,128)(2,1)} custom-call(bf16[4,8,224,128]{3,2,1,0:T(8,128)(2,1)} %bitcast.52), custom_call_target="tpu_custom_call" | custom-call | tf_op jit(solution)/shard_map/pallas_call | solution.py:118
  47.3 6.2 %fusion.7 = bf16[512,128]{0,1:T(8,128)(2,1)S(1)} fusion(bf16[7168,128]{1,0:T(8,128)(2,1)} %bitcast.49, bf16[512,7168]{1,0:T(8,128)(2,1)} %param.8), kind=kOutput, calls=%fused_computation.14 | convolution fusion | flops 939589632 | bytes 9306112 | tf_op jit(solution)/shard_map/dot_general | solution.py:251
  54.3 14.8 %shard_map.78 = bf16[2,2,2,128,128]{4,3,2,1,0:T(8,128)(2,1)} custom-call(bf16[2,2,128,128]{3,2,1,0:T(8,128)(2,1)} %bitcast.67), custom_call_target="tpu_custom_call" | custom-call | tf_op jit(solution)/shard_map/pallas_call | solution.py:174
  69.2 1.7 broadcast_in_dim.23
  71.6 3.9 %shard_map.79 = bf16[40,128,128]{2,1,0:T(8,128)(2,1)} custom-call(s32[2,40]{1,0:T(2,128)} %select_reduce_fusion.idx_ref, bf16[8,128,128]{2,1,0:T(8,128)(2,1)} %bitcast.64, f32[40,128,128]{2,1,0:T(8,128)} %bitcast.7.given_ref), custom_call_target="tpu_custom_call" | custom-call | tf_op jit(solution)/shard_map/pallas_call | solution.py:253
  75.5 21.1 %shard_map.80 = bf16[4,8,160,128]{3,2,1,0:T(8,128)(2,1)} custom-call(bf16[4,8,160,128]{3,2,1,0:T(8,128)(2,1)} %bitcast.57), custom_call_target="tpu_custom_call" | custom-call | tf_op jit(solution)/shard_map/pallas_call | solution.py:118
  96.6 12.4 %fusion.4 = bf16[2560,128]{0,1:T(8,128)(2,1)S(1)} fusion(bf16[5120,128]{1,0:T(8,128)(2,1)} %bitcast.54, bf16[5120,2560]{1,0:T(8,128)(2,1)} %param.7), kind=kOutput, calls=%fused_computation.9 | convolution fusion | flops 3355770880 | bytes 28180480 | tf_op jit(solution)/shard_map/dot_general | solution.py:267
  109.1 1.1 copy.26
  110.2 28.1 %shard_map.81 = bf16[4,4,160,128]{3,2,1,0:T(8,128)(2,1)} custom-call(bf16[4,4,160,128]{3,2,1,0:T(8,128)(2,1)} %bitcast.61), custom_call_target="tpu_custom_call" | custom-call | tf_op jit(solution)/shard_map/pallas_call | solution.py:118
  138.3 13.8 %fusion.2 = bf16[5120,128]{0,1:T(8,128)(2,1)S(1)} fusion(bf16[2560,128]{1,0:T(8,128)(2,1)} %bitcast.60, bf16[5120,2560]{1,0:T(8,128)(2,1)} %param.7), kind=kOutput, calls=%fused_computation.5 | convolution fusion | flops 3356098560 | bytes 28180480 | tf_op jit(solution)/shard_map/dot_general | solution.py:273
  152.1 1.4 copy.27
  153.5 21.5 %shard_map.82 = bf16[4,8,160,128]{3,2,1,0:T(8,128)(2,1)} custom-call(bf16[4,8,160,128]{3,2,1,0:T(8,128)(2,1)} %bitcast.58), custom_call_target="tpu_custom_call" | custom-call | tf_op jit(solution)/shard_map/pallas_call | solution.py:118
  175.1 2.1 shard_map.83
  177.2 18.4 %shard_map.84 = bf16[1,4,256,128]{3,2,1,0:T(8,128)(2,1)} custom-call(bf16[1,4,256,128]{3,2,1,0:T(8,128)(2,1)} %bitcast.65), custom_call_target="tpu_custom_call" | custom-call | tf_op jit(solution)/shard_map/pallas_call | solution.py:118
  195.6 1.7 dynamic-slice_convert_fusion
  197.3 4.3 %fusion = bf16[7168,128]{0,1:T(8,128)(2,1)S(1)} fusion(bf16[512,7168]{1,0:T(8,128)(2,1)} %param.8, bf16[1024,128]{1,0:T(8,128)(2,1)} %bitcast.66, s32[]{:T(128)S(6)} %select_n.33), kind=kOutput, calls=%fused_computation.2 | convolution fusion | flops 940441600 | bytes 9306116 | tf_op jit(solution)/shard_map/dot_general | solution.py:291
  201.6 2.3 copy.28
  203.9 24.5 %shard_map.85 = bf16[4,8,224,128]{3,2,1,0:T(8,128)(2,1)} custom-call(bf16[4,8,224,128]{3,2,1,0:T(8,128)(2,1)} %bitcast.53), custom_call_target="tpu_custom_call" | custom-call | tf_op jit(solution)/shard_map/pallas_call | solution.py:118
  228.5 12.4 %fusion.5 = bf16[1792,128]{0,1:T(8,128)(2,1)S(1)} fusion(bf16[7168,1792]{1,0:T(8,128)(2,1)} %param.6, bf16[7168,128]{1,0:T(8,128)(2,1)} %bitcast.51, bf16[7168,128]{1,0:T(8,128)(2,1)S(1)} %bitcast.50), kind=kOutput, calls=%fused_computation.11 | convolution fusion | flops 3292233728 | bytes 29818880 | tf_op jit(solution)/shard_map/dot_general | solution.py:299
  241.9 25.4 %shard_map.86 = bf16[2,4,2,224,128]{4,3,2,1,0:T(8,128)(2,1)} custom-call(bf16[4,2,224,128]{3,2,1,0:T(8,128)(2,1)} %bitcast.63), custom_call_target="tpu_custom_call" | custom-call | tf_op jit(solution)/shard_map/pallas_call | solution.py:174
  267.3 1.4 bitcast_convert_fusion
  268.7 7.8 %copy.33 = f32[2,1792,128]{2,0,1:T(2,128)} copy(f32[2,1792,128]{2,1,0:T(8,128)S(1)} %bitcast_convert_fusion) | data formatting | bytes 3670016 | tf_op jit(solution)/shard_map/convert_element_type | solution.py:303
  (15 shorter events, 5.4 us)
Async XLA Ops:
  0.6 2.2 copy-start
  53.6 17.3 %copy-start.3 = (f32[640,128]{1,0:T(8,128)S(1)}, f32[640,128]{1,0:T(8,128)}, u32[]{:S(2)}) copy-start(f32[640,128]{1,0:T(8,128)} %param.10) | copy-start | bytes 983044
  203.9 24.6 %copy-start.2 = (bf16[4,8,224,128]{3,2,1,0:T(8,128)(2,1)S(1)}, bf16[4,8,224,128]{3,2,1,0:T(8,128)(2,1)}, u32[]{:S(2)}) copy-start(bf16[4,8,224,128]{3,2,1,0:T(8,128)(2,1)} %shard_map.77) | copy-start | bytes 5505028
  267.3 9.2 %copy-start.1 = (f32[1792,2,128]{2,1,0:T(2,128)S(1)}, f32[1792,2,128]{2,1,0:T(2,128)}, u32[]{:S(2)}) copy-start(f32[1792,2,128]{2,1,0:T(2,128)} %param.9) | copy-start | bytes 5505028

commit v3 on v2

--- a/solution.py
+++ b/solution.py
@@ -210,6 +210,18 @@
     lax.fori_loop(0, o_ref.shape[0], body, 0)
 
 
+def weave_kernel(x_ref, o_ref):
+    step = 64
+
+    def body(i, _):
+        rows = pl.ds(pl.multiple_of(i * step, step), step)
+        for k in range(2):
+            o_ref[rows, k, :] = x_ref[k, rows, :].astype(jnp.float32)
+        return 0
+
+    lax.fori_loop(0, o_ref.shape[0] // step, body, 0)
+
+
 def local(row_devices, col_devices, child_inverse, root_upper, coupling, child_rhs, root_rhs, child_map):
     row_place = lax.axis_index("row")
     col_place = lax.axis_index("col")
@@ -300,7 +312,12 @@
         child_inverse, adjusted, contract_first, preferred_element_type=jnp.float32
     )
     final_both = both_sum(final_rows.astype(jnp.bfloat16), "row", row_devices, 4, 7)
-    child_solution = jnp.transpose(final_both, (1, 0, 2)).astype(jnp.float32)
+    child_solution = pl.pallas_call(
+        weave_kernel,
+        out_shape=jax.ShapeDtypeStruct(child_rhs.shape, jnp.float32),
+        in_specs=[vmem],
+        out_specs=vmem,
+    )(final_both)
     return (root_solution, child_solution)
 
 

time: 277 us -> 272 us (0.982)
  local copies, waits for them, and re-layouts: 20.5 us -> 12.7 us
  Pallas kernels: 188 us -> 192 us
    convert_element_type x1 -> x0, local copies, waits for them, and re-layouts: 7.79 us -> none  [local(): child_solution = jnp.transpose(final_both, (1, 0, 2)).astype(jnp.float32)]
    pallas_call x0 -> x1, Pallas kernels: none -> 3.64 us  [local(): pl.pallas_call(weave_kernel, out_shape=jax.ShapeDtypeStruct(child_rhs.sha...]
where the time goes in v3:
time: 272 us
  Pallas kernels  192 us (71%)
  matrix products  63.3 us (23%)
  local copies, waits for them, and re-layouts  12.7 us (5%)
  other arithmetic  3.21 us (1%)
    pallas_call x6, Pallas kernels, all_sum(): pl.pallas_call(functools.partial(all_sum_kernel, axis, n, orders, gathers...  141 us
    pallas_call x2, Pallas kernels, both_sum(): pl.pallas_call(functools.partial(both_sum_kernel, axis, n, streams), out_...  40.7 us
    dot_general x1, matrix products, local(): jnp.dot(root_upper, solved_low, preferred_element_type=jnp.float32)  13.8 us
    dot_general x1, matrix products, local(): jnp.dot(child_inverse, own_rhs, preferred_element_type=jnp.float32)  13.3 us
    dot_general x1, matrix products, local(): lax.dot_general(child_inverse, adjusted, contract_first, preferred_elemen...  13.1 us
    dot_general x1, matrix products, local(): lax.dot_general(root_upper, root_low, contract_first, preferred_element_t...  12.5 us
    dot_general x1, matrix products, local(): update = jnp.dot(coupling, child_low, preferred_element_type=jnp.float32)  6.22 us

profile of v3, /device:TPU:0, one launch (start us, length us, event | category | flops | bytes accessed | tf_op | source)
XLA Modules:
  0.0 271.6 jit_solution(7877114734274956369)
XLA Ops:
  3.6 13.3 %fusion.1 = bf16[7168,128]{0,1:T(8,128)(2,1)S(1)} fusion(bf16[7168,1792]{1,0:T(8,128)(2,1)} %param.6, f32[1792,1,128]{2,0,1:T(8,128)S(1)} %bitcast.54), kind=kOutput, calls=%fused_computation.3 | convolution fusion | flops 3289481216 | bytes 28442624 | tf_op jit(solution)/shard_map/dot_general | solution.py:260
  17.0 2.3 copy.22
  19.3 28.0 %shard_map.77 = bf16[4,8,224,128]{3,2,1,0:T(8,128)(2,1)} custom-call(bf16[4,8,224,128]{3,2,1,0:T(8,128)(2,1)} %bitcast.47), custom_call_target="tpu_custom_call" | custom-call | tf_op jit(solution)/shard_map/pallas_call | solution.py:118
  47.3 6.2 %fusion.7 = bf16[512,128]{0,1:T(8,128)(2,1)S(1)} fusion(bf16[7168,128]{1,0:T(8,128)(2,1)} %bitcast.44, bf16[512,7168]{1,0:T(8,128)(2,1)} %param.8), kind=kOutput, calls=%fused_computation.13 | convolution fusion | flops 939589632 | bytes 9306112 | tf_op jit(solution)/shard_map/dot_general | solution.py:263
  54.3 14.8 %shard_map.78 = bf16[2,2,2,128,128]{4,3,2,1,0:T(8,128)(2,1)} custom-call(bf16[2,2,128,128]{3,2,1,0:T(8,128)(2,1)} %bitcast.62), custom_call_target="tpu_custom_call" | custom-call | tf_op jit(solution)/shard_map/pallas_call | solution.py:174
  69.2 1.7 broadcast_in_dim.23
  71.6 3.9 %shard_map.79 = bf16[40,128,128]{2,1,0:T(8,128)(2,1)} custom-call(s32[2,40]{1,0:T(2,128)} %select_reduce_fusion.idx_ref, bf16[8,128,128]{2,1,0:T(8,128)(2,1)} %bitcast.59, f32[40,128,128]{2,1,0:T(8,128)} %bitcast.7.given_ref), custom_call_target="tpu_custom_call" | custom-call | tf_op jit(solution)/shard_map/pallas_call | solution.py:265
  75.5 21.1 %shard_map.80 = bf16[4,8,160,128]{3,2,1,0:T(8,128)(2,1)} custom-call(bf16[4,8,160,128]{3,2,1,0:T(8,128)(2,1)} %bitcast.52), custom_call_target="tpu_custom_call" | custom-call | tf_op jit(solution)/shard_map/pallas_call | solution.py:118
  96.6 12.5 %fusion.4 = bf16[2560,128]{0,1:T(8,128)(2,1)S(1)} fusion(bf16[5120,128]{1,0:T(8,128)(2,1)} %bitcast.49, bf16[5120,2560]{1,0:T(8,128)(2,1)} %param.7), kind=kOutput, calls=%fused_computation.9 | convolution fusion | flops 3355770880 | bytes 28180480 | tf_op jit(solution)/shard_map/dot_general | solution.py:279
  109.1 1.1 copy.24
  110.2 27.7 %shard_map.81 = bf16[4,4,160,128]{3,2,1,0:T(8,128)(2,1)} custom-call(bf16[4,4,160,128]{3,2,1,0:T(8,128)(2,1)} %bitcast.57), custom_call_target="tpu_custom_call" | custom-call | tf_op jit(solution)/shard_map/pallas_call | solution.py:118
  137.9 13.8 %fusion.2 = bf16[5120,128]{0,1:T(8,128)(2,1)S(1)} fusion(bf16[2560,128]{1,0:T(8,128)(2,1)} %bitcast.55, bf16[5120,2560]{1,0:T(8,128)(2,1)} %param.7), kind=kOutput, calls=%fused_computation.5 | convolution fusion | flops 3356098560 | bytes 28180480 | tf_op jit(solution)/shard_map/dot_general | solution.py:285
  151.8 1.4 copy.25
  153.2 21.7 %shard_map.82 = bf16[4,8,160,128]{3,2,1,0:T(8,128)(2,1)} custom-call(bf16[4,8,160,128]{3,2,1,0:T(8,128)(2,1)} %bitcast.53), custom_call_target="tpu_custom_call" | custom-call | tf_op jit(solution)/shard_map/pallas_call | solution.py:118
  174.9 2.1 shard_map.83
  177.1 18.3 %shard_map.84 = bf16[1,4,256,128]{3,2,1,0:T(8,128)(2,1)} custom-call(bf16[1,4,256,128]{3,2,1,0:T(8,128)(2,1)} %bitcast.60), custom_call_target="tpu_custom_call" | custom-call | tf_op jit(solution)/shard_map/pallas_call | solution.py:118
  195.4 1.7 dynamic-slice_convert_fusion
  197.1 4.3 %fusion = bf16[7168,128]{0,1:T(8,128)(2,1)S(1)} fusion(bf16[512,7168]{1,0:T(8,128)(2,1)} %param.8, bf16[1024,128]{1,0:T(8,128)(2,1)} %bitcast.61, s32[]{:T(128)S(6)} %select_n.33), kind=kOutput, calls=%fused_computation.2 | convolution fusion | flops 940441600 | bytes 9306116 | tf_op jit(solution)/shard_map/dot_general | solution.py:303
  201.4 2.3 copy.26
  203.7 24.3 %shard_map.85 = bf16[4,8,224,128]{3,2,1,0:T(8,128)(2,1)} custom-call(bf16[4,8,224,128]{3,2,1,0:T(8,128)(2,1)} %bitcast.48), custom_call_target="tpu_custom_call" | custom-call | tf_op jit(solution)/shard_map/pallas_call | solution.py:118
  228.0 13.1 %fusion.5 = bf16[1792,128]{0,1:T(8,128)(2,1)S(1)} fusion(bf16[7168,1792]{1,0:T(8,128)(2,1)} %param.6, bf16[7168,128]{1,0:T(8,128)(2,1)} %bitcast.46, bf16[7168,128]{1,0:T(8,128)(2,1)} %bitcast.45), kind=kOutput, calls=%fused_computation.11 | convolution fusion | flops 3292233728 | bytes 29818880 | tf_op jit(solution)/shard_map/dot_general | solution.py:311
  241.1 1.0 copy.27
  242.1 25.8 %shard_map.86 = bf16[2,4,2,224,128]{4,3,2,1,0:T(8,128)(2,1)} custom-call(bf16[4,2,224,128]{3,2,1,0:T(8,128)(2,1)} %bitcast.58), custom_call_target="tpu_custom_call" | custom-call | tf_op jit(solution)/shard_map/pallas_call | solution.py:174
  267.9 3.6 %shard_map.87 = f32[1792,2,128]{2,1,0:T(2,128)} custom-call(bf16[2,1792,128]{2,1,0:T(8,128)(2,1)} %bitcast.56), custom_call_target="tpu_custom_call" | custom-call | tf_op jit(solution)/shard_map/pallas_call | solution.py:315
  (12 shorter events, 4.5 us)
Async XLA Ops:
  0.6 2.2 copy-start
  53.6 17.3 %copy-start.2 = (f32[640,128]{1,0:T(8,128)S(1)}, f32[640,128]{1,0:T(8,128)}, u32[]{:S(2)}) copy-start(f32[640,128]{1,0:T(8,128)} %param.10) | copy-start | bytes 983044
  228.0 43.6 %copy-start.1 = (f32[1792,2,128]{2,1,0:T(2,128)S(1)}, f32[1792,2,128]{2,1,0:T(2,128)}, u32[]{:S(2)}) copy-start(f32[1792,2,128]{2,1,0:T(2,128)} %param.9) | copy-start | bytes 5505028
